TPU v7x, 32 devices: a whole 2x2x4 slice. The times are simulated.
32 devices in a mesh: groups: 2 (over x), ep: 16 (over z, y, core).
Axes of the slice: x: 2, y: 2, z: 4, core: 2. Of those that a mesh axis runs over, the one named last changes fastest.
Arguments:
- tokens: bfloat16 [512, 3072], P(('groups', 'ep')), parts along dimension 0, may hold values from -6 to 6
- routes: int32 [512, 2], P(('groups', 'ep')), parts along dimension 0, may hold values from 0 to 3, all different within a row
- route_weights: float32 [512, 2], P(('groups', 'ep')), parts along dimension 0, may hold values from 0.1 to 1
- live_counts: int32 [32], P(('groups', 'ep')), parts along dimension 0, may hold values from 8 to 16, as said below
- w_gate: bfloat16 [3072, 32768], P(None, 'ep'), may hold values from -0.109375 to 0.109375
- w_up: bfloat16 [3072, 32768], P(None, 'ep'), may hold values from -0.109375 to 0.109375
- w_down: bfloat16 [32768, 3072], P('ep'), may hold values from -0.0625 to 0.0625
Outputs:
- mixed: bfloat16 [512, 3072], P(('groups', 'ep')), parts along dimension 0
There are 2 independent parts, one for each index of `groups`. A program takes and returns all parts, laid end to end along the dimension named above; an argument that names none is the same for every part. Nothing has to cross between parts.
Inputs may be any that keep to these rules, and one draw needn't show every extreme that they name: `routes`: each token names two different experts. The live tokens of a device are its first live_counts rows; some device has all 16 live and some has 8.
All inputs are finite; a program needn't handle non-finite values.
Results may differ from a plain program's by a relative error of at most 0.0057.
Values may be sent and summed in bfloat16 or wider, within the bound.
A program may use at most 128 MiB of HBM per device.

v0:
```python
import jax
import jax.numpy as jnp
from jax import lax
from jax.sharding import PartitionSpec as P

EXPERTS = 4


def expert_rows(row_block, w_gate, w_up, w_down):
    gate = jnp.dot(row_block, w_gate, preferred_element_type=jnp.float32)
    upward = jnp.dot(row_block, w_up, preferred_element_type=jnp.float32)
    hidden = (jax.nn.silu(gate) * upward).astype(jnp.bfloat16)
    return jnp.dot(hidden, w_down, preferred_element_type=jnp.float32).astype(jnp.bfloat16)


def local(tokens, routes, route_weights, live_counts, w_gate, w_up, w_down):
    devices = lax.axis_size("ep")
    partners = devices // EXPERTS
    tok_rows, features = tokens.shape
    all_rows = devices * tok_rows
    is_live = jnp.arange(tok_rows, dtype=jnp.int32) < live_counts[0]
    chosen = (routes[:, :, None] == jnp.arange(EXPERTS, dtype=jnp.int32)[None, None, :]) & is_live[
        :, None, None
    ]
    assigned = chosen.reshape(tok_rows * 2, EXPERTS).astype(jnp.int32)
    earlier = jnp.cumsum(assigned, axis=0) - assigned
    slot_index = jnp.sum(earlier * assigned, axis=1).reshape(tok_rows, 2)
    target = jnp.where(is_live[:, None], routes * tok_rows + slot_index, -1)
    select = jnp.any(
        jnp.arange(EXPERTS * tok_rows, dtype=jnp.int32)[:, None, None] == target[None, :, :], axis=2
    )
    outbox = jnp.dot(
        select.astype(jnp.bfloat16), tokens, preferred_element_type=jnp.float32
    ).astype(jnp.bfloat16)
    outbox = outbox.reshape(EXPERTS, tok_rows, features)
    outgoing = jnp.broadcast_to(outbox[:, None], (EXPERTS, partners, tok_rows, features)).reshape(
        devices, tok_rows, features
    )
    received = lax.all_to_all(outgoing, "ep", split_axis=0, concat_axis=0, tiled=True)
    flat_rows = received.reshape(all_rows, features)
    partial_value = expert_rows(flat_rows, w_gate, w_up, w_down)
    returned = lax.all_to_all(
        partial_value.reshape(devices, tok_rows, features),
        "ep",
        split_axis=0,
        concat_axis=0,
        tiled=True,
    )
    summed = jnp.sum(
        returned.reshape(EXPERTS, partners, tok_rows, features).astype(jnp.float32), axis=1
    )
    gathered = summed.reshape(EXPERTS * tok_rows, features)
    picked = gathered[jnp.maximum(target, 0)]
    mixed = (
        route_weights[:, 0][:, None] * picked[:, 0] + route_weights[:, 1][:, None] * picked[:, 1]
    )
    mixed = jnp.where(is_live[:, None], mixed, jnp.float32(0.0))
    return mixed.astype(jnp.bfloat16)


def solution(mesh):
    in_specs = (
        P(("groups", "ep"), None),
        P(("groups", "ep"), None),
        P(("groups", "ep"), None),
        P(("groups", "ep")),
        P(None, "ep"),
        P(None, "ep"),
        P("ep", None),
    )
    out_specs = P(("groups", "ep"), None)
    return jax.shard_map(local, mesh=mesh, in_specs=in_specs, out_specs=out_specs, check_vma=False)
```

profile of v0, /device:TPU:15, one launch (start us, length us, event | category | flops | bytes accessed | tf_op | source)
XLA Modules:
  0.0 114.2 jit_solution(10619593889007973785)
XLA Ops:
  0.7 0.1 broadcast_in_dim.42.clone
  0.8 0.1 and.11
  0.9 0.8 copy.24
  1.6 0.1 eq.30
  1.7 0.1 fusion.8
  1.9 0.2 select_reduce_fusion
  2.0 0.1 reshape.33
  2.1 0.1 copy.26
  2.2 0.7 broadcast_maximum_fusion
  2.9 0.1 fusion.6
  3.0 0.3 convolution_convert_fusion.1
  3.3 0.2 broadcast_in_dim.45
  3.5 42.4 %all_to_all.10 = bf16[16,16,3072]{2,1,0:T(8,128)(2,1)S(1)} all-to-all(bf16[16,16,3072]{2,1,0:T(8,128)(2,1)S(1)} %bitcast.38), channel_id=1, replica_groups=mesh['groups'=2,'ep'=16] {'ep'}, dimensions={0} | all-to-all | bytes 3145728 | tf_op jit(solution)/shard_map/all_to_all | solution.py:39
  45.9 7.8 %fusion.11 = f32[256,2048]{1,0:T(8,128)} fusion(bf16[256,3072]{1,0:T(8,128)(2,1)S(1)} %bitcast.39, bf16[3072,2048]{1,0:T(8,128)(2,1)} %param.11), kind=kOutput, calls=%fused_computation.27 | convolution fusion | flops 3221225472 | bytes 16252928 | tf_op jit(solution)/shard_map/dot_general | solution.py:10
  53.7 16.9 %convolution_convert_fusion = bf16[256,3072]{1,0:T(8,128)(2,1)} fusion(bf16[2048,3072]{1,0:T(8,128)(2,1)} %param.13, bf16[256,3072]{1,0:T(8,128)(2,1)S(1)} %bitcast.40, bf16[3072,2048]{1,0:T(8,128)(2,1)} %param.12, f32[256,2048]{1,0:T(8,128)} %fusion.11), kind=kOutput, calls=%fused_computation.1 | convolution fusion | flops 6446383104 | bytes 30408704 | tf_op jit(solution)/shard_map/dot_general | solution.py:13
  70.6 5.2 %all-to-all-start.1 = ((bf16[16,16,3072]{2,1,0:T(8,128)(2,1)}), bf16[16,16,3072]{2,1,0:T(8,128)(2,1)S(1)}, u32[]{:S(2)}, u32[]{:S(2)}) async-start(bf16[16,16,3072]{2,1,0:T(8,128)(2,1)} %bitcast.5), calls=%async_computation.1 | async-start | bytes 3145728 | tf_op jit(solution)/shard_map/all_to_all | solution.py:42
  75.7 0.1 copy.27
  75.8 0.1 reshape.41
  76.0 36.0 %all-to-all-done.1 = bf16[16,16,3072]{2,1,0:T(8,128)(2,1)S(1)} async-done(((bf16[16,16,3072]{2,1,0:T(8,128)(2,1)}), bf16[16,16,3072]{2,1,0:T(8,128)(2,1)S(1)}, u32[]{:S(2)}, u32[]{:S(2)}) %all-to-all-start.1) | async-done | bytes 1572896 | tf_op jit(solution)/shard_map/all_to_all | solution.py:42
  111.9 0.2 convert_reduce_fusion
  112.2 0.7 gather_fusion
  112.9 0.2 reshape.40
  113.1 0.3 fusion.10
  113.4 0.8 fusion.4
  (8 shorter events, 0.1 us)
Async XLA Ops:
  0.0 3.0 %copy-start = (bf16[16,3072]{1,0:T(8,128)(2,1)S(1)}, bf16[16,3072]{1,0:T(8,128)(2,1)}, u32[]{:S(2)}) copy-start(bf16[16,3072]{1,0:T(8,128)(2,1)} %param.7) | copy-start | bytes 294916
  70.6 5.4 %copy-start.1 = (f32[16,2]{0,1:T(2,128)S(1)}, f32[16,2]{0,1:T(2,128)}, u32[]{:S(2)}) copy-start(f32[16,2]{0,1:T(2,128)} %param.9) | copy-start | bytes 388
  70.6 41.4 %all-to-all-start.1 = ((bf16[16,16,3072]{2,1,0:T(8,128)(2,1)}), bf16[16,16,3072]{2,1,0:T(8,128)(2,1)S(1)}, u32[]{:S(2)}, u32[]{:S(2)}) async-start(bf16[16,16,3072]{2,1,0:T(8,128)(2,1)} %bitcast.5), calls=%async_computation.1 | async-start | bytes 3145728 | tf_op jit(solution)/shard_map/all_to_all | solution.py:42
where the time goes:
time: 114 us
  blocking collectives  42.4 us (37%)
  waiting for transfers between devices  36 us (32%)
  matrix products  25 us (22%)
  starting transfers between devices  5.18 us (5%)
  local copies, waits for them, and re-layouts  2.77 us (2%)
  other arithmetic  2.13 us (2%)
    all_to_all x1, blocking collectives, local(): lax.all_to_all(outgoing, 'ep', split_axis=0, concat_axis=0, tiled=True)  42.4 us
    all_to_all x1, waiting for transfers between devices, local(): lax.all_to_all(partial_value.reshape(devices, tok_rows, features), 'ep',...  36 us
    dot_general x1, matrix products, expert_rows(): jnp.dot(hidden, w_down, preferred_element_type=jnp.float32)  16.9 us
    dot_general x1, matrix products, expert_rows(): gate = jnp.dot(row_block, w_gate, preferred_element_type=jnp.float32)  7.78 us
    all_to_all x1, starting transfers between devices, local(): lax.all_to_all(partial_value.reshape(devices, tok_rows, features), 'ep',...  5.18 us
  transfers between devices with their start and end apart: 1, of which 1 were waited for; matrix products, arithmetic and copies ran while one was open for 0% of the time, Pallas kernels for 0%

commit v1 on v0

v1 whole, which is shorter than its diff:
```python
import functools

import jax
import jax.numpy as jnp
from jax import lax
from jax.experimental import pallas as pl
from jax.experimental.pallas import tpu as pltpu
from jax.sharding import PartitionSpec as P

MESH = pl.DeviceIdType.MESH
EXPERTS = 4
EXTRA = 128
TILE = 256


def remote(src, dst, send_sem, recv_sem, target):
    return pltpu.make_async_remote_copy(
        src_ref=src,
        dst_ref=dst,
        send_sem=send_sem,
        recv_sem=recv_sem,
        device_id={"ep": target},
        device_id_type=MESH,
    )


def kernel(
    n, columns, chunks,
    tok, routes, weights, live, wg_hbm, wu_hbm, wd_hbm, out,
    xb, wg, wu, wd, hid, row_w, pf, pb, sb, got_r, got_l, put_r, put_l,
    w_sem, d_sem, ag_ss, ag_rs, sib_ss, sib_rs, rs_ss, rs_rs, sx_ss, sx_rs,
):
    rows, feat = tok.shape
    chips = n // 2
    half = chips // 2
    me = lax.axis_index("ep")
    core, chip = me % 2, me // 2
    depth = chips // columns
    if columns == 2:
        y, z = chip % 2, chip // 2
        ring = (1 - y) * z + y * (chips - 1 - z)
    else:
        ring = chip

    def device_at(pos):
        pos = (pos + chips) % chips
        if columns == 2:
            y = pos // depth
            z = (1 - y) * pos + y * (chips - 1 - pos)
            where = z * 2 + y
        else:
            where = pos
        return where * 2 + core

    right, left, sibling = device_at(ring + 1), device_at(ring - 1), chip * 2 + (1 - core)

    hid_tiles = wg.shape[0]
    out_tiles = wd.shape[0]

    def w_copy(j, which):
        src, dst = ((wg_hbm, wg), (wu_hbm, wu))[which]
        cols = pl.ds(pl.multiple_of(j * TILE, TILE), TILE)
        return pltpu.make_async_copy(src.at[:, cols], dst.at[j], w_sem.at[which, j])

    def d_copy(j):
        cols = pl.ds(pl.multiple_of(j * TILE, TILE), TILE)
        return pltpu.make_async_copy(wd_hbm.at[:, cols], wd.at[j], d_sem.at[j])

    for j in range(hid_tiles):
        w_copy(j, 0).start()
        w_copy(j, 1).start()
    for j in range(out_tiles):
        d_copy(j).start()

    barrier = pltpu.get_barrier_semaphore()
    for peer in (right, left, sibling):
        pl.semaphore_signal(barrier, inc=1, device_id={"ep": peer}, device_id_type=MESH)

    def block(pos, side):
        pos = (pos + chips) % chips
        return pl.ds(pl.multiple_of((side * chips + pos) * rows, rows), rows)

    mine = block(ring, core)
    xb[mine, pl.ds(0, feat)] = tok[...]
    is_live = lax.broadcasted_iota(jnp.int32, (rows, EXTRA), 0) < live[0]
    lane = lax.broadcasted_iota(jnp.int32, (rows, EXTRA), 1)
    which_expert = lane % EXPERTS
    combined = jnp.zeros((rows, EXTRA), jnp.float32)
    for k in range(2):
        combined += jnp.where(
            (routes[:, k : k + 1] == which_expert) & is_live, weights[:, k : k + 1], 0.0
        )
    high = combined.astype(jnp.bfloat16).astype(jnp.float32)
    middle = (combined - high).astype(jnp.bfloat16).astype(jnp.float32)
    low = combined - high - middle
    term = lane // EXPERTS
    packed = jnp.where(term == 0, high, jnp.where(term == 1, middle, jnp.where(term == 2, low, 0.0)))
    xb[mine, pl.ds(feat, EXTRA)] = packed.astype(jnp.bfloat16)

    pl.semaphore_wait(barrier, 3)

    width = feat + EXTRA
    split = (width // 2 + 127) // 128 * 128
    spans = (pl.ds(0, split), pl.ds(split, width - split))
    sent = []

    def ag_send(direction, step):
        pos = ring - (step - 1) if direction == 0 else ring + (step - 1)
        where = block(pos, core)
        view = xb.at[where] if step < half else xb.at[where, spans[direction]]
        copy = remote(
            view, view, ag_ss.at[direction, step - 1], ag_rs.at[direction, step - 1],
            right if direction == 0 else left,
        )
        copy.start()
        sent.append(copy)

    def ag_wait(direction, step):
        pos = ring - step if direction == 0 else ring + step
        where = block(pos, core)
        view = xb.at[where] if step < half else xb.at[where, spans[direction]]
        remote(
            view, view, ag_ss.at[direction, step - 1], ag_rs.at[direction, step - 1],
            right if direction == 0 else left,
        ).wait_recv()

    def sib_copy(offset, side):
        view = xb.at[block(ring + offset, side)]
        slot = (offset + chips) % chips
        return remote(view, view, sib_ss.at[slot], sib_rs.at[slot], sibling)

    def sib_send(offset):
        copy = sib_copy(offset, core)
        copy.start()
        sent.append(copy)

    ag_send(0, 1)
    ag_send(1, 1)
    sib_send(0)
    for step in range(1, half + 1):
        for direction in range(2):
            ag_wait(direction, step)
            if step < half:
                ag_send(direction, step + 1)
                sib_send(step if direction == 1 else -step)
    sib_send(half)
    for offset in range(chips):
        sib_copy(offset, 1 - core).wait_recv()

    expert = me // (n // EXPERTS)
    tail = xb[:, pl.ds(feat, EXTRA)].astype(jnp.float32)
    lanes = lax.broadcasted_iota(jnp.int32, tail.shape, 1)
    row_w[...] = jnp.sum(
        jnp.where(lanes % EXPERTS == expert, tail, 0.0), axis=1, keepdims=True
    )

    def hidden_tile(j, carry):
        w_copy(j, 0).wait()
        w_copy(j, 1).wait()
        x = xb[:, pl.ds(0, feat)]
        gate = jnp.dot(x, wg[j], preferred_element_type=jnp.float32)
        upward = jnp.dot(x, wu[j], preferred_element_type=jnp.float32)
        hid[:, pl.ds(pl.multiple_of(j * TILE, TILE), TILE)] = (
            gate / (1.0 + jnp.exp(-gate)) * upward
        ).astype(jnp.bfloat16)
        return carry

    lax.fori_loop(0, hid_tiles, hidden_tile, 0)

    per_chunk = out_tiles // chunks
    chunk = per_chunk * TILE
    cut = (chunk // 2 + 127) // 128 * 128
    parts = (pl.ds(0, cut), pl.ds(cut, chunk - cut))
    side_rows = chips * rows

    def side_span(side):
        return pl.ds(pl.multiple_of(side * side_rows, side_rows), side_rows)

    def sx_copy(k):
        return remote(pb.at[k, side_span(1 - core)], sb.at[k], sx_ss.at[k], sx_rs.at[k], sibling)

    def local_sum(k, pos, cols):
        pos = (pos + chips) % chips
        return pf[k, block(pos, core), cols] + sb[
            k, pl.ds(pl.multiple_of(pos * rows, rows), rows), cols
        ].astype(jnp.float32)

    whole = pl.ds(0, chunk)

    def rs_copy(direction, k, step):
        src, dst = ((put_r, got_r), (put_l, got_l))[direction]
        src, dst = src.at[k, step - 1], dst.at[k, step - 1]
        if step == 1:
            src, dst = src.at[:, parts[direction]], dst.at[:, parts[direction]]
        return remote(
            src, dst, rs_ss.at[direction, k, step - 1], rs_rs.at[direction, k, step - 1],
            right if direction == 0 else left,
        )

    def rs_step(k, step):
        for direction in range(2):
            put, got = ((put_r, got_r), (put_l, got_l))[direction]
            away = half - step + 1
            pos = ring + away if direction == 0 else ring - away
            if step == 1:
                put[k, 0, :, parts[direction]] = local_sum(k, pos, parts[direction]).astype(jnp.bfloat16)
            else:
                rs_copy(direction, k, step - 1).wait_recv()
                if step == 2:
                    here, other = parts[direction], parts[1 - direction]
                    put[k, 1, :, here] = (
                        local_sum(k, pos, here) + got[k, 0, :, here].astype(jnp.float32)
                    ).astype(jnp.bfloat16)
                    put[k, 1, :, other] = local_sum(k, pos, other).astype(jnp.bfloat16)
                else:
                    put[k, step - 1] = (
                        local_sum(k, pos, whole) + got[k, step - 2].astype(jnp.float32)
                    ).astype(jnp.bfloat16)
            copy = rs_copy(direction, k, step)
            copy.start()
            sent.append(copy)

    def open_ring(k):
        sx_copy(k).wait_recv()
        rs_step(k, 1)

    for k in range(chunks):

        def out_tile(t, carry, k=k):
            j = k * per_chunk + t
            d_copy(j).wait()
            cols = pl.ds(pl.multiple_of(t * TILE, TILE), TILE)
            value = jnp.dot(hid[...], wd[j], preferred_element_type=jnp.float32) * row_w[...]
            pf[k, :, cols] = value
            pb[k, :, cols] = value.astype(jnp.bfloat16)
            return carry

        lax.fori_loop(0, per_chunk, out_tile, 0)
        copy = sx_copy(k)
        copy.start()
        sent.append(copy)
        if k > 0:
            open_ring(k - 1)
    open_ring(chunks - 1)
    for step in range(2, half + 1):
        for k in range(chunks):
            rs_step(k, step)
    for k in range(chunks):
        rs_copy(0, k, half).wait_recv()
        rs_copy(1, k, half).wait_recv()
        total = (
            local_sum(k, ring, whole)
            + got_r[k, half - 1].astype(jnp.float32)
            + got_l[k, half - 1].astype(jnp.float32)
        )
        out[:, pl.ds(k * chunk, chunk)] = total.astype(jnp.bfloat16)
    for copy in sent:
        copy.wait_send()


def local(n, tokens, routes, route_weights, live_counts, w_gate, w_up, w_down):
    rows, feat = tokens.shape
    share = w_gate.shape[1]
    chips = n // 2
    half = chips // 2
    columns = 2 if chips <= 8 else 1
    chunks = 3
    chunk = feat // chunks
    all_rows = n * rows
    vmem = pl.BlockSpec(memory_space=pltpu.VMEM)
    hbm = pl.BlockSpec(memory_space=pl.ANY)
    bf16, f32 = jnp.bfloat16, jnp.float32
    ring_buffer = pltpu.VMEM((chunks, half, rows, chunk), bf16)
    dma = pltpu.SemaphoreType.DMA
    return pl.pallas_call(
        functools.partial(kernel, n, columns, chunks),
        out_shape=jax.ShapeDtypeStruct((rows, feat), bf16),
        in_specs=[vmem, vmem, vmem, pl.BlockSpec(memory_space=pltpu.SMEM), hbm, hbm, hbm],
        out_specs=vmem,
        scratch_shapes=[
            pltpu.VMEM((all_rows, feat + EXTRA), bf16),
            pltpu.VMEM((share // TILE, feat, TILE), bf16),
            pltpu.VMEM((share // TILE, feat, TILE), bf16),
            pltpu.VMEM((feat // TILE, share, TILE), bf16),
            pltpu.VMEM((all_rows, share), bf16),
            pltpu.VMEM((all_rows, 1), f32),
            pltpu.VMEM((chunks, all_rows, chunk), f32),
            pltpu.VMEM((chunks, all_rows, chunk), bf16),
            pltpu.VMEM((chunks, chips * rows, chunk), bf16),
            ring_buffer, ring_buffer, ring_buffer, ring_buffer,
            dma((2, share // TILE)),
            dma((feat // TILE,)),
            dma((2, half)), dma((2, half)),
            dma((chips,)), dma((chips,)),
            dma((2, chunks, half)), dma((2, chunks, half)),
            dma((chunks,)), dma((chunks,)),
        ],
        compiler_params=pltpu.CompilerParams(
            collective_id=0, has_side_effects=True, vmem_limit_bytes=60 * 2**20
        ),
    )(tokens, routes, route_weights, live_counts, w_gate, w_up, w_down)


def solution(mesh):
    in_specs = (
        P(("groups", "ep"), None),
        P(("groups", "ep"), None),
        P(("groups", "ep"), None),
        P(("groups", "ep")),
        P(None, "ep"),
        P(None, "ep"),
        P("ep", None),
    )
    return jax.shard_map(
        functools.partial(local, mesh.shape["ep"]),
        mesh=mesh, in_specs=in_specs, out_specs=P(("groups", "ep"), None), check_vma=False,
    )
```

time: 114 us -> 55.1 us (0.48)
  the two profiles are of different devices: /device:TPU:15 before, /device:TPU:0 now
where the time goes in v1:
time: 55.1 us; the launch traced here: 54.9 us
  Pallas kernels  50 us (91%)
  local copies, waits for them, and re-layouts  4.24 us (8%)
  between operations  0.66 us (1%)
    pallas_call x1, Pallas kernels, local(): pl.pallas_call(functools.partial(kernel, n, columns, chunks), out_shape=j...  50 us
    unnamed x3, local copies, waits for them, and re-layouts  4.24 us

profile of v1, /device:TPU:0, one launch (start us, length us, event | category | flops | bytes accessed | tf_op | source)
XLA Modules:
  0.0 54.9 jit_solution(12900158560027762004)
XLA Ops:
  0.7 1.4 %copy.8.routes = s32[16,2]{1,0:T(8,128)} copy(s32[16,2]{0,1:T(2,128)} %param.8) | data formatting | bytes 256 | tf_op args[1]
  2.0 1.3 %copy.9.weights = f32[16,2]{1,0:T(8,128)} copy(f32[16,2]{0,1:T(2,128)} %param.9) | data formatting | bytes 256 | tf_op args[2]
  3.4 50.0 %shard_map.73 = bf16[16,3072]{1,0:T(8,128)(2,1)} custom-call(bf16[16,3072]{1,0:T(8,128)(2,1)} %tok.1, s32[16,2]{1,0:T(8,128)} %copy.8.routes, f32[16,2]{1,0:T(8,128)} %copy.9.weights, s32[1]{0:T(128)S(6)} %copy.11.live, bf16[3072,2048]{1,0:T(8,128)(2,1)} %wg_hbm.1, bf16[3072,2048]{1,0:T(8,128)(2,1)} %wu_hbm.1, bf16[2048,3072]{1,0:T(8,128)(2,1)} %wd_hbm.1), custom_call_target="tpu_custom_call" | custom-call | tf_op jit(solution)/shard_map/pallas_call | solution.py:275
  53.3 1.5 %copy.12 = bf16[16,3072]{1,0:T(8,128)(2,1)} copy(bf16[16,3072]{1,0:T(8,128)(2,1)} %shard_map.73) | data formatting | bytes 196608

commit v2 on v1

v2 whole, which is shorter than its diff:
```python
import functools

import jax
import jax.numpy as jnp
from jax import lax
from jax.experimental import pallas as pl
from jax.experimental.pallas import tpu as pltpu
from jax.sharding import PartitionSpec as P

MESH = pl.DeviceIdType.MESH
EXPERTS = 4
EXTRA = 128
TILE = 256


def remote(src, dst, send_sem, recv_sem, target):
    return pltpu.make_async_remote_copy(
        src_ref=src,
        dst_ref=dst,
        send_sem=send_sem,
        recv_sem=recv_sem,
        device_id={"ep": target},
        device_id_type=MESH,
    )


def kernel(
    n, columns, chunks,
    tok, routes, weights, live, wg_hbm, wu_hbm, wd_hbm, out,
    xb, wg, wu, wd, hid, row_w, pf, pb, sb, got_r, got_l, put_r, put_l,
    w_sem, d_sem, ag_ss, ag_rs, sib_ss, sib_rs, rs_ss, rs_rs, sx_ss, sx_rs,
):
    rows, feat = tok.shape
    chips = n // 2
    half = chips // 2
    me = lax.axis_index("ep")
    core, chip = me % 2, me // 2
    depth = chips // columns
    if columns == 2:
        y, z = chip % 2, chip // 2
        ring = (1 - y) * z + y * (chips - 1 - z)
    else:
        ring = chip

    def device_at(pos):
        pos = (pos + chips) % chips
        if columns == 2:
            y = pos // depth
            z = (1 - y) * pos + y * (chips - 1 - pos)
            where = z * 2 + y
        else:
            where = pos
        return where * 2 + core

    right, left, sibling = device_at(ring + 1), device_at(ring - 1), chip * 2 + (1 - core)

    hid_tiles = wg.shape[0]
    out_tiles = wd.shape[0]

    def w_copy(j, which):
        src, dst = ((wg_hbm, wg), (wu_hbm, wu))[which]
        cols = pl.ds(pl.multiple_of(j * TILE, TILE), TILE)
        return pltpu.make_async_copy(src.at[:, cols], dst.at[j], w_sem.at[which, j])

    def d_copy(j):
        cols = pl.ds(pl.multiple_of(j * TILE, TILE), TILE)
        return pltpu.make_async_copy(wd_hbm.at[:, cols], wd.at[j], d_sem.at[j])

    for j in range(hid_tiles):
        w_copy(j, 0).start()
        w_copy(j, 1).start()
    for j in range(out_tiles):
        d_copy(j).start()

    barrier = pltpu.get_barrier_semaphore()
    for peer in (right, left, sibling):
        pl.semaphore_signal(barrier, inc=1, device_id={"ep": peer}, device_id_type=MESH)

    near = half // 2
    groups = (
        [d for d in range(-near, near + 1)],
        [d for d in range(near + 1, half)] + [half] + [-d for d in range(near + 1, half)],
    )
    counts = [len(g) * rows for g in groups]
    starts = [0, 2 * counts[0]]

    def home(rel):
        rel = half if rel == -half else rel
        g = 0 if rel in groups[0] else 1
        return g, groups[g].index(rel)

    def slot(rel, side):
        g, i = home(rel)
        return pl.ds(starts[g] + side * counts[g] + i * rows, rows)

    def side_row(rel):
        g, i = home(rel)
        return pl.ds((counts[0] if g else 0) + i * rows, rows)

    xb[slot(0, 0), pl.ds(0, feat)] = tok[...]
    diagonal = lax.broadcasted_iota(jnp.int32, (rows, rows), 0) == lax.broadcasted_iota(
        jnp.int32, (rows, rows), 1
    )

    def column(ref, k):
        spread = jnp.broadcast_to(ref[k : k + 1, :].astype(jnp.float32), (rows, rows))
        return jnp.sum(jnp.where(diagonal, spread, 0.0), axis=1, keepdims=True)

    is_live = lax.broadcasted_iota(jnp.int32, (rows, EXTRA), 0) < live[0]
    lane = lax.broadcasted_iota(jnp.int32, (rows, EXTRA), 1)
    which_expert = lane % EXPERTS
    combined = jnp.zeros((rows, EXTRA), jnp.float32)
    for k in range(2):
        combined += jnp.where(
            (column(routes, k).astype(jnp.int32) == which_expert) & is_live, column(weights, k), 0.0
        )
    high = combined.astype(jnp.bfloat16).astype(jnp.float32)
    middle = (combined - high).astype(jnp.bfloat16).astype(jnp.float32)
    low = combined - high - middle
    term = lane // EXPERTS
    packed = jnp.where(term == 0, high, jnp.where(term == 1, middle, jnp.where(term == 2, low, 0.0)))
    xb[slot(0, 0), pl.ds(feat, EXTRA)] = packed.astype(jnp.bfloat16)

    pl.semaphore_wait(barrier, 3)

    width = feat + EXTRA
    split = (width // 2 + 127) // 128 * 128
    spans = (pl.ds(0, split), pl.ds(split, width - split))
    sent = []

    def go(copy):
        copy.start()
        sent.append(copy)

    def ag_copy(direction, step):
        sign = -1 if direction == 0 else 1
        src, dst = slot(sign * (step - 1), 0), slot(sign * step, 0)
        if step == half:
            src, dst = (src, spans[direction]), (dst, spans[direction])
        return remote(
            xb.at[src], xb.at[dst], ag_ss.at[direction, step - 1], ag_rs.at[direction, step - 1],
            right if direction == 0 else left,
        )

    def sib_copy(rel):
        i = rel % chips
        return remote(xb.at[slot(rel, 0)], xb.at[slot(rel, 1)], sib_ss.at[i], sib_rs.at[i], sibling)

    def ag_step(step):
        for direction in range(2):
            ag_copy(direction, step).wait_recv()
            if step < half:
                go(ag_copy(direction, step + 1))
                go(sib_copy(-step if direction == 0 else step))
        if step == half:
            go(sib_copy(half))

    expert = me // (n // EXPERTS)
    spots = [pl.ds(starts[g], 2 * counts[g]) for g in range(2)]

    def weigh(g):
        for rel in groups[g]:
            sib_copy(rel).wait_recv()
        tail = xb[spots[g], pl.ds(feat, EXTRA)].astype(jnp.float32)
        lanes = lax.broadcasted_iota(jnp.int32, tail.shape, 1)
        row_w[spots[g], :] = jnp.sum(
            jnp.where(lanes % EXPERTS == expert, tail, 0.0), axis=1, keepdims=True
        )

    def hidden_tiles(g, first, last):
        def tile(j, carry):
            if g == 0:
                w_copy(j, 0).wait()
                w_copy(j, 1).wait()
            x = xb[spots[g], pl.ds(0, feat)]
            gate = jnp.dot(x, wg[j], preferred_element_type=jnp.float32)
            upward = jnp.dot(x, wu[j], preferred_element_type=jnp.float32)
            hid[spots[g], pl.ds(pl.multiple_of(j * TILE, TILE), TILE)] = (
                gate / (1.0 + jnp.exp(-gate)) * upward
            ).astype(jnp.bfloat16)
            return carry

        if last > first:
            lax.fori_loop(first, last, tile, 0)

    go(ag_copy(0, 1))
    go(ag_copy(1, 1))
    go(sib_copy(0))
    for step in range(1, near + 1):
        ag_step(step)
    weigh(0)
    late = half - near
    for i in range(late):
        hidden_tiles(0, i * hid_tiles // late, (i + 1) * hid_tiles // late)
        ag_step(near + 1 + i)
    weigh(1)
    hidden_tiles(1, 0, hid_tiles)

    per_chunk = out_tiles // chunks
    chunk = per_chunk * TILE
    cut = (chunk // 2 + 127) // 128 * 128
    parts = (pl.ds(0, cut), pl.ds(cut, chunk - cut))
    whole = pl.ds(0, chunk)
    side_spots = (pl.ds(0, counts[0]), pl.ds(counts[0], counts[1]))

    def sx_copy(k, g):
        return remote(
            pb.at[k, side_spots[g]], sb.at[k, side_spots[g]], sx_ss.at[k, g], sx_rs.at[k, g], sibling
        )

    def out_tiles_of(k, g):
        def tile(t, carry):
            j = k * per_chunk + t
            if g == 1:
                d_copy(j).wait()
            cols = pl.ds(pl.multiple_of(t * TILE, TILE), TILE)
            value = jnp.dot(
                hid[spots[g], :], wd[j], preferred_element_type=jnp.float32
            ) * row_w[spots[g], :]
            pf[k, side_spots[g], cols] = value[: counts[g]]
            pb[k, side_spots[g], cols] = value[counts[g] :].astype(jnp.bfloat16)
            return carry

        lax.fori_loop(0, per_chunk, tile, 0)
        go(sx_copy(k, g))

    def local_sum(k, rel, cols):
        return pf[k, side_row(rel), cols] + sb[k, side_row(rel), cols].astype(jnp.float32)

    def rs_copy(direction, k, step):
        src, dst = ((put_r, got_r), (put_l, got_l))[direction]
        src, dst = src.at[k, step - 1], dst.at[k, step - 1]
        if step == 1:
            src, dst = src.at[:, parts[direction]], dst.at[:, parts[direction]]
        return remote(
            src, dst, rs_ss.at[direction, k, step - 1], rs_rs.at[direction, k, step - 1],
            right if direction == 0 else left,
        )

    def rs_step(k, step):
        for direction in range(2):
            put, got = ((put_r, got_r), (put_l, got_l))[direction]
            away = half - step + 1
            rel = away if direction == 0 else -away
            if step == 1:
                put[k, 0, :, parts[direction]] = local_sum(k, rel, parts[direction]).astype(jnp.bfloat16)
            else:
                rs_copy(direction, k, step - 1).wait_recv()
                if step == 2:
                    here, other = parts[direction], parts[1 - direction]
                    put[k, 1, :, here] = (
                        local_sum(k, rel, here) + got[k, 0, :, here].astype(jnp.float32)
                    ).astype(jnp.bfloat16)
                    put[k, 1, :, other] = local_sum(k, rel, other).astype(jnp.bfloat16)
                else:
                    put[k, step - 1] = (
                        local_sum(k, rel, whole) + got[k, step - 2].astype(jnp.float32)
                    ).astype(jnp.bfloat16)
            go(rs_copy(direction, k, step))

    def open_ring(k):
        sx_copy(k, 1).wait_recv()
        rs_step(k, 1)

    for k in range(chunks):
        out_tiles_of(k, 1)
        if k > 0:
            open_ring(k - 1)
    out_tiles_of(0, 0)
    open_ring(chunks - 1)
    for k in range(1, chunks):
        out_tiles_of(k, 0)
        rs_step(k - 1, 2)
    rs_step(chunks - 1, 2)
    for k in range(chunks):
        sx_copy(k, 0).wait_recv()
    for step in range(3, half + 1):
        for k in range(chunks):
            rs_step(k, step)
    for k in range(chunks):
        rs_copy(0, k, half).wait_recv()
        rs_copy(1, k, half).wait_recv()
        total = (
            local_sum(k, 0, whole)
            + got_r[k, half - 1].astype(jnp.float32)
            + got_l[k, half - 1].astype(jnp.float32)
        )
        out[:, pl.ds(k * chunk, chunk)] = total.astype(jnp.bfloat16)
    for copy in sent:
        copy.wait_send()


def local(n, tokens, routes, route_weights, live_counts, w_gate, w_up, w_down):
    rows, feat = tokens.shape
    share = w_gate.shape[1]
    chips = n // 2
    half = chips // 2
    columns = 2 if chips <= 8 else 1
    chunks = 3
    chunk = feat // chunks
    all_rows = n * rows
    vmem = pl.BlockSpec(memory_space=pltpu.VMEM)
    hbm = pl.BlockSpec(memory_space=pl.ANY)
    bf16, f32 = jnp.bfloat16, jnp.float32
    ring_buffer = pltpu.VMEM((chunks, half, rows, chunk), bf16)
    dma = pltpu.SemaphoreType.DMA
    return pl.pallas_call(
        functools.partial(kernel, n, columns, chunks),
        out_shape=jax.ShapeDtypeStruct((rows, feat), bf16),
        in_specs=[vmem, vmem, vmem, pl.BlockSpec(memory_space=pltpu.SMEM), hbm, hbm, hbm],
        out_specs=vmem,
        scratch_shapes=[
            pltpu.VMEM((all_rows, feat + EXTRA), bf16),
            pltpu.VMEM((share // TILE, feat, TILE), bf16),
            pltpu.VMEM((share // TILE, feat, TILE), bf16),
            pltpu.VMEM((feat // TILE, share, TILE), bf16),
            pltpu.VMEM((all_rows, share), bf16),
            pltpu.VMEM((all_rows, 1), f32),
            pltpu.VMEM((chunks, chips * rows, chunk), f32),
            pltpu.VMEM((chunks, chips * rows, chunk), bf16),
            pltpu.VMEM((chunks, chips * rows, chunk), bf16),
            ring_buffer, ring_buffer, ring_buffer, ring_buffer,
            dma((2, share // TILE)),
            dma((feat // TILE,)),
            dma((2, half)), dma((2, half)),
            dma((chips,)), dma((chips,)),
            dma((2, chunks, half)), dma((2, chunks, half)),
            dma((chunks, 2)), dma((chunks, 2)),
        ],
        compiler_params=pltpu.CompilerParams(
            collective_id=0, has_side_effects=True, vmem_limit_bytes=60 * 2**20
        ),
    )(tokens, routes.T, route_weights.T, live_counts, w_gate, w_up, w_down)


def solution(mesh):
    in_specs = (
        P(("groups", "ep"), None),
        P(("groups", "ep"), None),
        P(("groups", "ep"), None),
        P(("groups", "ep")),
        P(None, "ep"),
        P(None, "ep"),
        P("ep", None),
    )
    return jax.shard_map(
        functools.partial(local, mesh.shape["ep"]),
        mesh=mesh, in_specs=in_specs, out_specs=P(("groups", "ep"), None), check_vma=False,
    )
```

time: 55.1 us -> 49.1 us (0.89)
  Pallas kernels: 50 us -> 46.7 us
  local copies, waits for them, and re-layouts: 4.24 us -> 1.54 us
    pallas_call x1, Pallas kernels: 50 us -> 46.7 us  [local(): pl.pallas_call(functools.partial(kernel, n, columns, chunks), out_shape=j...]
    unnamed x3 -> x1, local copies, waits for them, and re-layouts: 4.24 us -> 1.54 us
where the time goes in v2:
time: 49.1 us; the launch traced here: 48.9 us
  Pallas kernels  46.7 us (95%)
  local copies, waits for them, and re-layouts  1.54 us (3%)
  between operations  0.66 us (1%)
    pallas_call x1, Pallas kernels, local(): pl.pallas_call(functools.partial(kernel, n, columns, chunks), out_shape=j...  46.7 us
    unnamed x1, local copies, waits for them, and re-layouts  1.54 us

profile of v2, /device:TPU:0, one launch (start us, length us, event | category | flops | bytes accessed | tf_op | source)
XLA Modules:
  0.0 48.9 jit_solution(12638469090502326506)
XLA Ops:
  0.7 46.7 %shard_map.73 = bf16[16,3072]{1,0:T(8,128)(2,1)} custom-call(bf16[16,3072]{1,0:T(8,128)(2,1)} %tok.1, s32[2,16]{1,0:T(2,128)} %bitcast.2, f32[2,16]{1,0:T(2,128)} %bitcast.3, s32[1]{0:T(128)S(6)} %copy.9.live, bf16[3072,2048]{1,0:T(8,128)(2,1)} %wg_hbm.1, bf16[3072,2048]{1,0:T(8,128)(2,1)} %wu_hbm.1, bf16[2048,3072]{1,0:T(8,128)(2,1)} %wd_hbm.1), custom_call_target="tpu_custom_call" | custom-call | tf_op jit(solution)/shard_map/pallas_call | solution.py:307
  47.4 1.5 %copy.10 = bf16[16,3072]{1,0:T(8,128)(2,1)} copy(bf16[16,3072]{1,0:T(8,128)(2,1)} %shard_map.73) | data formatting | bytes 196608

commit v3 on v2

--- a/solution.py
+++ b/solution.py
@@ -52,7 +52,11 @@
             where = pos
         return where * 2 + core
 
-    right, left, sibling = device_at(ring + 1), device_at(ring - 1), chip * 2 + (1 - core)
+    sibling = chip * 2 + (1 - core)
+    ahead = (
+        (device_at(ring + 1), device_at(ring + 2)),
+        (device_at(ring - 1), device_at(ring - 2)),
+    )
 
     hid_tiles = wg.shape[0]
     out_tiles = wd.shape[0]
@@ -73,7 +77,7 @@
         d_copy(j).start()
 
     barrier = pltpu.get_barrier_semaphore()
-    for peer in (right, left, sibling):
+    for peer in ahead[0] + ahead[1] + (sibling,):
         pl.semaphore_signal(barrier, inc=1, device_id={"ep": peer}, device_id_type=MESH)
 
     near = half // 2
@@ -121,7 +125,7 @@
     packed = jnp.where(term == 0, high, jnp.where(term == 1, middle, jnp.where(term == 2, low, 0.0)))
     xb[slot(0, 0), pl.ds(feat, EXTRA)] = packed.astype(jnp.bfloat16)
 
-    pl.semaphore_wait(barrier, 3)
+    pl.semaphore_wait(barrier, 5)
 
     width = feat + EXTRA
     split = (width // 2 + 127) // 128 * 128
@@ -139,7 +143,7 @@
             src, dst = (src, spans[direction]), (dst, spans[direction])
         return remote(
             xb.at[src], xb.at[dst], ag_ss.at[direction, step - 1], ag_rs.at[direction, step - 1],
-            right if direction == 0 else left,
+            ahead[direction][0],
         )
 
     def sib_copy(rel):
@@ -227,64 +231,67 @@
     def local_sum(k, rel, cols):
         return pf[k, side_row(rel), cols] + sb[k, side_row(rel), cols].astype(jnp.float32)
 
-    def rs_copy(direction, k, step):
+    def rs_copy(direction, k, away):
         src, dst = ((put_r, got_r), (put_l, got_l))[direction]
-        src, dst = src.at[k, step - 1], dst.at[k, step - 1]
-        if step == 1:
+        src, dst = src.at[k, away - 1], dst.at[k, away - 1]
+        if away == half:
             src, dst = src.at[:, parts[direction]], dst.at[:, parts[direction]]
         return remote(
-            src, dst, rs_ss.at[direction, k, step - 1], rs_rs.at[direction, k, step - 1],
-            right if direction == 0 else left,
-        )
-
-    def rs_step(k, step):
+            src, dst, rs_ss.at[direction, k, away - 1], rs_rs.at[direction, k, away - 1],
+            ahead[direction][1 - away % 2],
+        )
+
+    def rs_send(k, away):
         for direction in range(2):
             put, got = ((put_r, got_r), (put_l, got_l))[direction]
-            away = half - step + 1
             rel = away if direction == 0 else -away
-            if step == 1:
-                put[k, 0, :, parts[direction]] = local_sum(k, rel, parts[direction]).astype(jnp.bfloat16)
+            here, other = parts[direction], parts[1 - direction]
+            if away == half:
+                put[k, away - 1, :, here] = local_sum(k, rel, here).astype(jnp.bfloat16)
+            elif away % 2 == 1:
+                put[k, away - 1] = local_sum(k, rel, whole).astype(jnp.bfloat16)
             else:
-                rs_copy(direction, k, step - 1).wait_recv()
-                if step == 2:
-                    here, other = parts[direction], parts[1 - direction]
-                    put[k, 1, :, here] = (
-                        local_sum(k, rel, here) + got[k, 0, :, here].astype(jnp.float32)
-                    ).astype(jnp.bfloat16)
-                    put[k, 1, :, other] = local_sum(k, rel, other).astype(jnp.bfloat16)
-                else:
-                    put[k, step - 1] = (
-                        local_sum(k, rel, whole) + got[k, step - 2].astype(jnp.float32)
-                    ).astype(jnp.bfloat16)
-            go(rs_copy(direction, k, step))
-
-    def open_ring(k):
-        sx_copy(k, 1).wait_recv()
-        rs_step(k, 1)
+                rs_copy(direction, k, away + 1).wait_recv()
+                rs_copy(direction, k, away + 2).wait_recv()
+                for cols in (here, other):
+                    value = local_sum(k, rel, cols) + got[k, away, :, cols].astype(jnp.float32)
+                    if away + 2 < half or cols is here:
+                        value += got[k, away + 1, :, cols].astype(jnp.float32)
+                    put[k, away - 1, :, cols] = value.astype(jnp.bfloat16)
+            go(rs_copy(direction, k, away))
+
+    def rs_group(k, g):
+        sx_copy(k, g).wait_recv()
+        members = [d for d in groups[g] if d > 0]
+        if half in members:
+            rs_send(k, half)
+        for away in sorted(d for d in members if d % 2 == 1):
+            rs_send(k, away)
+
+    def rs_relay(k, g):
+        for away in sorted((d for d in groups[g] if 0 < d < half and d % 2 == 0), reverse=True):
+            rs_send(k, away)
 
     for k in range(chunks):
         out_tiles_of(k, 1)
         if k > 0:
-            open_ring(k - 1)
+            rs_group(k - 1, 1)
     out_tiles_of(0, 0)
-    open_ring(chunks - 1)
+    rs_group(chunks - 1, 1)
     for k in range(1, chunks):
         out_tiles_of(k, 0)
-        rs_step(k - 1, 2)
-    rs_step(chunks - 1, 2)
+        rs_group(k - 1, 0)
+        rs_relay(k - 1, 1)
+        rs_relay(k - 1, 0)
+    rs_group(chunks - 1, 0)
+    rs_relay(chunks - 1, 1)
+    rs_relay(chunks - 1, 0)
     for k in range(chunks):
-        sx_copy(k, 0).wait_recv()
-    for step in range(3, half + 1):
-        for k in range(chunks):
-            rs_step(k, step)
-    for k in range(chunks):
-        rs_copy(0, k, half).wait_recv()
-        rs_copy(1, k, half).wait_recv()
-        total = (
-            local_sum(k, 0, whole)
-            + got_r[k, half - 1].astype(jnp.float32)
-            + got_l[k, half - 1].astype(jnp.float32)
-        )
+        total = local_sum(k, 0, whole)
+        for direction in range(2):
+            for away in (1, 2):
+                rs_copy(direction, k, away).wait_recv()
+                total += (got_r, got_l)[direction][k, away - 1].astype(jnp.float32)
         out[:, pl.ds(k * chunk, chunk)] = total.astype(jnp.bfloat16)
     for copy in sent:
         copy.wait_send()

time: 49.1 us -> 47.1 us (0.959)
  Pallas kernels: 46.7 us -> 44.7 us
    pallas_call x1, Pallas kernels: 46.7 us -> 44.7 us  [local(): pl.pallas_call(functools.partial(kernel, n, columns, chunks), out_shape=j...]
where the time goes in v3:
time: 47.1 us; the launch traced here: 46.9 us
  Pallas kernels  44.7 us (95%)
  local copies, waits for them, and re-layouts  1.54 us (3%)
  between operations  0.66 us (1%)
    pallas_call x1, Pallas kernels, local(): pl.pallas_call(functools.partial(kernel, n, columns, chunks), out_shape=j...  44.7 us
    unnamed x1, local copies, waits for them, and re-layouts  1.54 us

profile of v3, /device:TPU:0, one launch (start us, length us, event | category | flops | bytes accessed | tf_op | source)
XLA Modules:
  0.0 46.9 jit_solution(3347980145549100567)
XLA Ops:
  0.7 44.7 %shard_map.73 = bf16[16,3072]{1,0:T(8,128)(2,1)} custom-call(bf16[16,3072]{1,0:T(8,128)(2,1)} %tok.1, s32[2,16]{1,0:T(2,128)} %bitcast.2, f32[2,16]{1,0:T(2,128)} %bitcast.3, s32[1]{0:T(128)S(6)} %copy.9.live, bf16[3072,2048]{1,0:T(8,128)(2,1)} %wg_hbm.1, bf16[3072,2048]{1,0:T(8,128)(2,1)} %wu_hbm.1, bf16[2048,3072]{1,0:T(8,128)(2,1)} %wd_hbm.1), custom_call_target="tpu_custom_call" | custom-call | tf_op jit(solution)/shard_map/pallas_call | solution.py:314
  45.4 1.5 %copy.10 = bf16[16,3072]{1,0:T(8,128)(2,1)} copy(bf16[16,3072]{1,0:T(8,128)(2,1)} %shard_map.73) | data formatting | bytes 196608
